TPU v7x, 512 devices: a whole 4x8x8 slice. The times are simulated.
512 devices in a mesh: tile: 128 (over z_lo, y, x, core), layer: 4 (over z_hi).
Axes of the slice: x: 4, y: 8, z: 8 (z_hi: 4, z_lo: 2; z = z_hi * 2 + z_lo), core: 2. Of those that a mesh axis runs over, the one named last changes fastest.
Arguments:
- rand_vectors: bfloat16 [4, 16, 1572864], P(None, None, ('tile', 'layer')), may hold values from -4 to 4
- onsite: bfloat16 [12288, 128, 128], P(('tile', 'layer')), as said below
- down_hop: bfloat16 [12288, 128, 128], P(('tile', 'layer')), may hold values from -0.1875 to 0.1875
- right_hop: bfloat16 [12288, 128, 128], P(('tile', 'layer')), may hold values from -0.1875 to 0.1875
- pattern: int32 [12288, 2], P(('tile', 'layer')), may hold values 0 or 1
- pairing: float32 [1572864], P(('tile', 'layer')), may hold values from 0.1 to 1
- link_rows: int32 [65536, 8], P(('tile', 'layer')), may hold values from 0 to 3071
- link_target: int32 [65536, 8], P(('tile', 'layer')), may hold values from 0 to 3071
- link_weight: bfloat16 [65536, 8], P(('tile', 'layer')), may hold values from -3 to 3
- link_count: int32 [65536], P(('tile', 'layer')), may hold values from 0 to 8, as said below
Outputs:
- cheb_one: float32 [4, 16, 1572864], P(None, None, ('tile', 'layer'))
- cheb_two: float32 [4, 16, 1572864], P(None, None, ('tile', 'layer'))
- moments: float32 [3, 4, 1572864], P(None, None, ('tile', 'layer'))
Inputs may be any that keep to these rules, and one draw needn't show every extreme that they name: `onsite`: every tile is symmetric. `link_rows`: a local site of the sending device. `link_target`: a local site of the receiving device. `link_count`: the number of used slots from one source tile row index to one receiving device; loads differ strongly between receiving tile row indices.
All inputs are finite; a program needn't handle non-finite values. No bound on the sum of `pattern` on one device may be relied on, other than what follows from the above.
Results may differ from a plain program's by a relative error of at most 0.0025.
Values may be sent and summed in bfloat16 or wider, within the bound.
No kernel may reach another device: no remote copies, remote signals or barrier semaphores. Data moves between devices by JAX's collectives and lax.ppermute only.
A program may use at most 64 MiB of HBM per device.

v0:
```python
import jax
import jax.numpy as jnp
from jax import lax
from jax.sharding import PartitionSpec as P

TILE = 128
TR = 4
TC = 6


def passed_along(value, axis, by):
    length = lax.axis_size(axis)
    pairs = [(i, i + by) for i in range(length) if 0 <= i + by < length]
    return lax.ppermute(value, axis, pairs)


def partner_2(value, axis, bit):
    return lax.ppermute(value, axis, [(i, i ^ 1 << bit) for i in range(lax.axis_size(axis))])


def with_halo(block, sides, width):
    for axis, dim in sides:
        count = lax.axis_size(axis)
        forward = [(i, i + 1) for i in range(count - 1)]
        backward = [(target, source) for source, target in forward]
        low = lax.ppermute(
            lax.slice_in_dim(block, block.shape[dim] - width, None, axis=dim), axis, forward
        )
        high = lax.ppermute(lax.slice_in_dim(block, 0, width, axis=dim), axis, backward)
        block = jnp.concatenate([low, block, high], axis=dim)
    return block


def hop_forward(tiles, field_grid):
    return jnp.einsum("rkij,nrkj->nrki", tiles, field_grid, preferred_element_type=jnp.float32)


def hop_transposed(tiles, field_grid):
    return jnp.einsum("rkji,nrkj->nrki", tiles, field_grid, preferred_element_type=jnp.float32)


def shards(
    rand_vectors,
    onsite,
    down_hop,
    right_hop,
    pattern,
    pairing,
    link_rows,
    link_target,
    link_weight,
    link_count,
):
    components, vectors, sites_dev = rand_vectors.shape
    field_rows = components * vectors
    tile_count = lax.axis_size("tile")
    slot_count = link_rows.shape[1]
    self_tiles = onsite.reshape(TR, TC, TILE, TILE)
    down_mask = (down_hop * pattern[:, 0][:, None, None].astype(jnp.bfloat16)).reshape(
        TR, TC, TILE, TILE
    )
    right_mask = (right_hop * pattern[:, 1][:, None, None].astype(jnp.bfloat16)).reshape(
        TR, TC, TILE, TILE
    )
    is_left = lax.axis_index("layer") % 2 == 0
    slot_live = jnp.arange(slot_count, dtype=jnp.int32)[None, :] < link_count[:, None]
    slot_weight = jnp.where(slot_live, link_weight.astype(jnp.float32), 0.0).reshape(-1)
    send_rows = link_rows.reshape(-1)
    recv_sites = link_target.reshape(-1)
    upper_blocks = passed_along(down_mask[TR - 1], "tile", 1)
    shifted_down = jnp.concatenate([upper_blocks[None], down_mask[:-1]], axis=0)
    weight_table = slot_weight.reshape(tile_count, slot_count).astype(jnp.bfloat16)
    weight_spread = lax.all_to_all(weight_table, "tile", split_axis=0, concat_axis=0, tiled=True)
    sender_weight = partner_2(weight_spread, "layer", 1).astype(jnp.float32).reshape(-1)

    def apply_hop(field_b):
        field_grid = field_b.reshape(field_rows, TR, TC, TILE)
        accumulated = hop_forward(self_tiles, field_grid)
        padded = with_halo(field_grid, (("tile", 1),), 1)
        accumulated = (
            accumulated
            + hop_forward(down_mask, padded[:, 2:])
            + hop_transposed(shifted_down, padded[:, :-2])
        )
        leftward = hop_transposed(right_mask, field_grid)
        payload = jnp.where(
            is_left, leftward[:, :, TC - 1], field_grid[:, :, 0].astype(jnp.float32)
        )
        partner = partner_2(payload, "layer", 0)
        right_edge = jnp.where(is_left, partner, 0.0).astype(jnp.bfloat16)
        accumulated = accumulated + hop_forward(
            right_mask, jnp.concatenate([field_grid[:, :, 1:], right_edge[:, :, None]], axis=2)
        )
        left_edge = jnp.where(is_left, 0.0, partner)
        accumulated = accumulated + jnp.concatenate(
            [left_edge[:, :, None], leftward[:, :, :-1]], axis=2
        )
        accumulated = accumulated.reshape(field_rows, sites_dev)
        flat_field = field_b.reshape(field_rows, sites_dev)
        outgoing = jnp.take(flat_field, send_rows, axis=1).reshape(
            field_rows, tile_count, slot_count
        )
        own_ends = jnp.take(flat_field, recv_sites, axis=1).reshape(
            field_rows, tile_count, slot_count
        )
        paired = jnp.concatenate([outgoing, own_ends], axis=2)
        paired_spread = lax.all_to_all(paired, "tile", split_axis=1, concat_axis=1, tiled=True)
        landed = partner_2(paired_spread, "layer", 1)
        arrived_terms = (
            landed[:, :, :slot_count].reshape(field_rows, -1).astype(jnp.float32)
            * slot_weight[None, :]
        )
        accumulated = accumulated.at[:, recv_sites].add(arrived_terms)
        returned_terms = (
            landed[:, :, slot_count:].reshape(field_rows, -1).astype(jnp.float32)
            * sender_weight[None, :]
        )
        accumulated = accumulated.at[:, send_rows].add(returned_terms)
        return accumulated.reshape(components, vectors, sites_dev)

    nambu_sign = jnp.array([1.0, 1.0, -1.0, -1.0], dtype=jnp.float32)[:, None, None]
    initial = rand_vectors.astype(jnp.float32)
    cheb_one = nambu_sign * apply_hop(rand_vectors) + pairing * jnp.roll(initial, 2, axis=0)
    one_rounded = cheb_one.astype(jnp.bfloat16)
    cheb_two = (
        2.0 * (nambu_sign * apply_hop(one_rounded) + pairing * jnp.roll(cheb_one, 2, axis=0))
        - initial
    )
    moments = jnp.stack(
        [
            jnp.mean(initial * initial, axis=1),
            jnp.mean(initial * cheb_one, axis=1),
            jnp.mean(initial * cheb_two, axis=1),
        ]
    )
    return (cheb_one, cheb_two, moments)


def solution(mesh):
    in_specs = (
        P(None, None, ("tile", "layer")),
        P(("tile", "layer"), None, None),
        P(("tile", "layer"), None, None),
        P(("tile", "layer"), None, None),
        P(("tile", "layer"), None),
        P(("tile", "layer")),
        P(("tile", "layer"), None),
        P(("tile", "layer"), None),
        P(("tile", "layer"), None),
        P(("tile", "layer")),
    )
    out_specs = (
        P(None, None, ("tile", "layer")),
        P(None, None, ("tile", "layer")),
        P(None, None, ("tile", "layer")),
    )
    return jax.shard_map(shards, mesh=mesh, in_specs=in_specs, out_specs=out_specs, check_vma=False)
```

profile of v0, /device:TPU:7, one launch (start us, length us, event | category | flops | bytes accessed | tf_op | source)
XLA Modules:
  0.0 250.8 jit_solution(17171188428479891034)
XLA Ops:
  0.7 1.6 reshape.197
  3.7 5.8 %collective-permute-start.3 = (f32[64,4,128]{2,0,1:T(8,128)}, f32[64,4,128]{2,0,1:T(8,128)}, u32[]{:S(2)}, u32[]{:S(2)}) collective-permute-start(f32[64,4,128]{2,0,1:T(8,128)} %fusion.54), channel_id=1, source_target_pairs={{0,1},{1,0},{2,3},{3,2},{4,5},{5,4},{6,7},{7,6},{8,9},{9,8},{10,11... | collective-permute-start | bytes 393224 | tf_op jit(solution)/shard_map/ppermute | solution.py:18
  10.2 2.9 %collective-permute-start = (bf16[64,1,6,128]{3,0,2,1:T(8,128)(2,1)}, bf16[64,1,6,128]{3,0,2,1:T(8,128)(2,1)}, u32[]{:S(2)}, u32[]{:S(2)}) collective-permute-start(bf16[64,1,6,128]{3,0,2,1:T(8,128)(2,1)} %get-tuple-element.17), channel_id=1, source_target_pairs={{4,0},{8,4},{12,8},{16,12},{20,16},{24,20},{28,24},{32,28},{36,32}... | collective-permute-start | bytes 294920 | tf_op jit(solution)/shard_map/ppermute | solution.py:29
  13.1 4.8 %collective-permute-start.1 = (bf16[64,1,6,128]{3,0,2,1:T(8,128)(2,1)}, bf16[64,1,6,128]{3,0,2,1:T(8,128)(2,1)}, u32[]{:S(2)}, u32[]{:S(2)}) collective-permute-start(bf16[64,1,6,128]{3,0,2,1:T(8,128)(2,1)} %get-tuple-element.16), channel_id=1, source_target_pairs={{0,4},{4,8},{8,12},{12,16},{16,20},{20,24},{24,28},{28,32},{32,36}... | collective-permute-start | bytes 294920 | tf_op jit(solution)/shard_map/ppermute | solution.py:26
  19.6 1.9 collective-permute-start.2
  22.3 13.1 %all-to-all-start.1 = ((bf16[128,1,8]{2,1,0:T(2,128)(2,1)}), bf16[128,1,8]{2,1,0:T(2,128)(2,1)S(1)}, u32[]{:S(2)}, u32[]{:S(2)}) async-start(bf16[128,1,8]{2,1,0:T(2,128)(2,1)} %copy.130), calls=%async_computation.1 | async-start | bytes 131072 | tf_op jit(solution)/shard_map/all_to_all | solution.py:73
  38.0 1.5 fusion.72
  39.9 3.2 %gather_fusion = bf16[1024,64]{1,0:T(8,128)(2,1)S(1)} fusion(bf16[64,3072]{0,1:T(8,128)(2,1)S(1)} %copy.124, s32[1024]{0:T(1024)S(1)} %fusion.57), kind=kCustom, calls=%fused_computation.clone | custom fusion | bytes 266240 | tf_op jit(solution)/shard_map/jit(_take)/gather | solution.py:100
  43.2 4.3 %gather_fusion.1 = bf16[1024,64]{1,0:T(8,128)(2,1)} fusion(bf16[64,3072]{0,1:T(8,128)(2,1)S(1)} %copy.124, s32[1024]{0:T(1024)S(1)} %fusion.58), kind=kCustom, calls=%fused_computation.1.clone | custom fusion | bytes 266240 | tf_op jit(solution)/shard_map/jit(_take)/gather | solution.py:103
  48.1 1.3 select_bitcast_fusion.2
  50.4 2.1 reshape.304
  52.5 12.9 %all-to-all-start = ((bf16[128,2,512]{2,1,0:T(2,128)(2,1)}), bf16[128,2,512]{2,1,0:T(2,128)(2,1)}, u32[]{:S(2)}, u32[]{:S(2)}) async-start(bf16[128,2,512]{2,1,0:T(2,128)(2,1)} %reshape.304), calls=%async_computation | async-start | bytes 524288 | tf_op jit(solution)/shard_map/all_to_all | solution.py:107
  66.1 7.9 %collective-permute-start.5 = (bf16[128,8]{0,1:T(8,128)(2,1)}, bf16[128,8]{0,1:T(8,128)(2,1)}, u32[]{:S(2)}, u32[]{:S(2)}) collective-permute-start(bf16[128,8]{0,1:T(8,128)(2,1)} %bitcast.27), channel_id=1, source_target_pairs={{0,2},{1,3},{2,0},{3,1},{4,6},{5,7},{6,4},{7,5},{8,10},{9,11},{10,... | collective-permute-start | bytes 6152 | tf_op jit(solution)/shard_map/ppermute | solution.py:18
  79.1 2.7 %convolution_add_fusion.3 = f32[4,6,64,128]{3,2,1,0:T(8,128)} fusion(f32[4,6,64,128]{3,2,1,0:T(8,128)} %fusion.72, bf16[4,6,128,128]{3,2,1,0:T(8,128)(2,1)S(1)} %bitcast.133, bf16[64,1,6,128]{3,0,2,1:T(8,128)(2,1)} %collective-permute-done, bf16[64,4,6,128]{3,0,2,1:T(8,128)(2,1)S(1)} %copy.110), kind=kOutput, calls=%fused_computation.20 | convolution fusion | flops 51511296 | bytes 2850816 | tf_op jit(solution)/shard_map/rkij,nrkj->nrki/dot_general | solution.py:35
  82.8 1.5 fusion.42
  84.4 2.2 reshape.305
  86.5 5.1 %collective-permute-start.4 = (bf16[64,128,16]{0,2,1:T(8,128)(2,1)}, bf16[64,128,16]{0,2,1:T(8,128)(2,1)}, u32[]{:S(2)}, u32[]{:S(2)}) collective-permute-start(bf16[64,128,16]{0,2,1:T(8,128)(2,1)} %bitcast.110), channel_id=1, source_target_pairs={{0,2},{1,3},{2,0},{3,1},{4,6},{5,7},{6,4},{7,5},{8,10},{9,11},{10,... | collective-permute-start | bytes 786440 | tf_op jit(solution)/shard_map/ppermute | solution.py:18
  91.7 2.9 %fusion.5 = f32[64,4,6,128]{3,0,2,1:T(8,128)} fusion(f32[4,6,64,128]{3,2,1,0:T(8,128)} %fusion.42, f32[4,6,64,128]{3,2,1,0:T(8,128)} %convolution_add_fusion.3, f32[64,4,5,128]{3,0,2,1:T(8,128)S(1)} %slice-done, f32[64,4,1,128]{3,0,2,1:T(8,128)S(1)} %select_bitcast_fusion.5, bf16[64,4,6,128]{3,0,2,1:T(8,128)(2,1)S(1)} %copy.110, ...), kind=kOutput, calls=%fused_computation.19 | convolution fusion | flops 53673984 | bytes 4423680 | tf_op jit(solution)/shard_map/rkji,nrkj->nrki/dot_general | solution.py:39
  94.6 1.6 copy.166
  96.2 20.6 %collective-permute-done.4 = bf16[64,128,16]{0,2,1:T(8,128)(2,1)} collective-permute-done((bf16[64,128,16]{0,2,1:T(8,128)(2,1)}, bf16[64,128,16]{0,2,1:T(8,128)(2,1)}, u32[]{:S(2)}, u32[]{:S(2)}) %collective-permute-start.4) | collective-permute-done | bytes 262176 | tf_op jit(solution)/shard_map/ppermute | solution.py:18
  116.8 7.1 %scatter_custom_fusion = f32[64,3072]{0,1:T(8,128)S(1)} fusion(f32[64,3072]{0,1:T(8,128)S(1)} %bitcast.126, s32[1024]{0:T(1024)} %bitcast.140, bf16[64,128,16]{0,2,1:T(8,128)(2,1)} %collective-permute-done.4, f32[1024]{0:T(1024)S(1)} %mul.125), kind=kCustom, calls=%fused_computation.54 | custom fusion | flops 196608 | bytes 1052672 | tf_op jit(solution)/shard_map/scatter-add | solution.py:113
  123.9 7.5 %scatter_custom_fusion.1 = f32[64,3072]{0,1:T(8,128)S(1)} fusion(f32[64,3072]{0,1:T(8,128)S(1)} %scatter_custom_fusion, s32[1024]{0:T(1024)} %bitcast.142, bf16[64,128,16]{0,2,1:T(8,128)(2,1)} %collective-permute-done.4, f32[1024]{0:T(1024)} %reshape.217), kind=kCustom, calls=%fused_computation.51 | custom fusion | flops 196608 | bytes 1052672 | tf_op jit(solution)/shard_map/scatter-add | solution.py:118
  131.4 1.3 copy.133
  132.7 2.6 %pad_maximum_fusion.1 = (f32[4,16,3072]{2,1,0:T(8,128)}, f32[4,16,3072]{2,1,0:T(8,128)}) fusion(f32[2,16,3072]{2,1,0:T(8,128)} %get-tuple-element.15, f32[2,16,3072]{2,1,0:T(8,128)} %get-tuple-element.14, f32[3072]{0:T(1024)S(1)} %copy-done.13, f32[4,16,3072]{2,1,0:T(8,128)} %bitcast.137, f32[4]{0:T(128)} %constant.42.clone), kind=kLoop, calls=%fused_computation.22 | loop fusion | flops 786432 | bytes 3158032 | tf_op jit(solution)/shard_map/jit(_roll_static)/concatenate | solution.py:123
  135.3 2.8 %copy.149 = f32[64,3072]{0,1:T(8,128)} copy(f32[64,3072]{1,0:T(8,128)} %bitcast.135) | data formatting | bytes 1572864 | tf_op jit(solution)/shard_map/jit(_roll_static)/concatenate | solution.py:123
  138.1 2.8 %add_convert_fusion = bf16[64,3072]{0,1:T(8,128)(2,1)} fusion(f32[64,3072]{0,1:T(8,128)} %copy.149, f32[64,3072]{0,1:T(8,128)S(1)} %scatter_custom_fusion.1, f32[3072]{0:T(1024)S(1)} %copy-done.13, f32[64]{0:T(128)} %mul.136), kind=kLoop, calls=%fused_computation.8 | loop fusion | flops 786432 | bytes 1978624 | tf_op jit(solution)/shard_map/convert_element_type | solution.py:124
  140.9 5.6 %gather_fusion.2 = bf16[1024,64]{1,0:T(8,128)(2,1)} fusion(bf16[64,3072]{0,1:T(8,128)(2,1)} %add_convert_fusion, s32[1024]{0:T(1024)} %copy-done.16), kind=kCustom, calls=%fused_computation.2.clone | custom fusion | bytes 266240 | tf_op jit(solution)/shard_map/jit(_take)/gather | solution.py:100
  146.5 5.6 %gather_fusion.3 = bf16[1024,64]{1,0:T(8,128)(2,1)} fusion(bf16[64,3072]{0,1:T(8,128)(2,1)} %add_convert_fusion, s32[1024]{0:T(1024)} %copy-done.15), kind=kCustom, calls=%fused_computation.3.clone | custom fusion | bytes 266240 | tf_op jit(solution)/shard_map/jit(_take)/gather | solution.py:103
  152.1 2.5 %concatenate.53 = f32[64,4,6,128]{3,2,1,0:T(8,128)} reshape(f32[4,16,3072]{2,1,0:T(8,128)} %get-tuple-element.8) | data formatting | bytes 1572864 | tf_op jit(solution)/shard_map/jit(_roll_static)/concatenate | solution.py:123
  154.7 1.3 copy.135
  156.0 2.0 fusion.14
  158.7 1.2 convolution_bitcast_fusion.1
  161.3 2.1 reshape.306
  163.4 13.8 %all-to-all-start.2 = ((bf16[128,2,512]{2,1,0:T(2,128)(2,1)}), bf16[128,2,512]{2,1,0:T(2,128)(2,1)}, u32[]{:S(2)}, u32[]{:S(2)}) async-start(bf16[128,2,512]{2,1,0:T(2,128)(2,1)} %reshape.306), calls=%async_computation.2 | async-start | bytes 524288 | tf_op jit(solution)/shard_map/all_to_all | solution.py:107
  177.2 2.3 collective-permute-start.6
  180.4 1.9 collective-permute-start.8
  182.4 5.6 %collective-permute-start.7 = (bf16[64,1,6,128]{3,0,1,2:T(8,128)(2,1)}, bf16[64,1,6,128]{3,0,1,2:T(8,128)(2,1)}, u32[]{:S(2)}, u32[]{:S(2)}) collective-permute-start(bf16[64,1,6,128]{3,0,1,2:T(8,128)(2,1)} %get-tuple-element.12), channel_id=1, source_target_pairs={{0,4},{4,8},{8,12},{12,16},{16,20},{20,24},{24,28},{28,32},{32,36}... | collective-permute-start | bytes 294920 | tf_op jit(solution)/shard_map/ppermute | solution.py:26
  190.9 1.5 convolution_add_fusion.1
  192.4 1.5 fusion.15
  194.6 2.1 reshape.307
  196.7 4.8 %collective-permute-start.9 = (bf16[64,128,16]{0,2,1:T(8,128)(2,1)}, bf16[64,128,16]{0,2,1:T(8,128)(2,1)}, u32[]{:S(2)}, u32[]{:S(2)}) collective-permute-start(bf16[64,128,16]{0,2,1:T(8,128)(2,1)} %bitcast.112), channel_id=1, source_target_pairs={{0,2},{1,3},{2,0},{3,1},{4,6},{5,7},{6,4},{7,5},{8,10},{9,11},{10,... | collective-permute-start | bytes 786440 | tf_op jit(solution)/shard_map/ppermute | solution.py:18
  201.6 2.2 fusion.2
  203.8 1.7 copy.169
  205.5 22.5 %collective-permute-done.9 = bf16[64,128,16]{0,2,1:T(8,128)(2,1)} collective-permute-done((bf16[64,128,16]{0,2,1:T(8,128)(2,1)}, bf16[64,128,16]{0,2,1:T(8,128)(2,1)}, u32[]{:S(2)}, u32[]{:S(2)}) %collective-permute-start.9) | collective-permute-done | bytes 262176 | tf_op jit(solution)/shard_map/ppermute | solution.py:18
  228.0 9.4 %scatter_custom_fusion.2 = f32[64,3072]{0,1:T(8,128)} fusion(f32[64,3072]{0,1:T(8,128)} %bitcast.136, s32[1024]{0:T(1024)} %bitcast.141, bf16[64,128,16]{0,2,1:T(8,128)(2,1)} %collective-permute-done.9, f32[1024]{0:T(1024)S(1)} %mul.125), kind=kCustom, calls=%fused_computation.48 | custom fusion | flops 196608 | bytes 1052672 | tf_op jit(solution)/shard_map/scatter-add | solution.py:113
  237.4 9.4 %scatter_custom_fusion.3 = f32[64,3072]{0,1:T(8,128)} fusion(f32[64,3072]{0,1:T(8,128)} %scatter_custom_fusion.2, s32[1024]{0:T(1024)} %bitcast.143, bf16[64,128,16]{0,2,1:T(8,128)(2,1)} %collective-permute-done.9, f32[1024]{0:T(1024)S(1)} %copy-done.14), kind=kCustom, calls=%fused_computation.45 | custom fusion | flops 196608 | bytes 1052672 | tf_op jit(solution)/shard_map/scatter-add | solution.py:118
  246.9 1.9 copy.151
  248.8 1.2 multiply_reduce_fusion.2
  (117 shorter events, 23.1 us)
Async XLA Ops:
  0.6 37.4 %copy-start = (bf16[24,128,128]{2,1,0:T(8,128)(2,1)S(1)}, bf16[24,128,128]{2,1,0:T(8,128)(2,1)}, u32[]{:S(2)}) copy-start(bf16[24,128,128]{2,1,0:T(8,128)(2,1)} %param.14) | copy-start | bytes 2359300
  0.6 1.8 copy-start.24
  0.7 1.8 copy-start.9
  2.6 15.3 %copy-start.10 = (bf16[24,128,128]{2,1,0:T(8,128)(2,1)S(1)}, bf16[24,128,128]{2,1,0:T(8,128)(2,1)}, u32[]{:S(2)}) copy-start(bf16[24,128,128]{2,1,0:T(8,128)(2,1)} %param.15) | copy-start | bytes 2359300
  3.0 14.9 %copy-start.6 = (f32[64,4,6,128]{3,0,2,1:T(8,128)}, f32[64,4,6,128]{3,0,2,1:T(8,128)S(1)}, u32[]{:S(2)}) copy-start(f32[64,4,6,128]{3,0,2,1:T(8,128)S(1)} %convolution_bitcast_fusion) | copy-start | bytes 2359300
  3.0 18.6 %copy-start.22 = (bf16[128,8]{0,1:T(8,128)(2,1)S(1)}, bf16[128,8]{0,1:T(8,128)(2,1)}, u32[]{:S(2)}) copy-start(bf16[128,8]{0,1:T(8,128)(2,1)} %param.21) | copy-start | bytes 6148
  3.0 18.6 %copy-start.23 = (s32[128]{0:T(128)S(1)}, s32[128]{0:T(128)}, u32[]{:S(2)}) copy-start(s32[128]{0:T(128)} %param.22) | copy-start | bytes 1540
  3.0 32.4 %copy-start.20 = (s32[128,8]{0,1:T(8,128)S(1)}, s32[128,8]{0,1:T(8,128)}, u32[]{:S(2)}) copy-start(s32[128,8]{0,1:T(8,128)} %param.20) | copy-start | bytes 12292
  3.0 33.2 %copy-start.21 = (s32[128,8]{0,1:T(8,128)S(1)}, s32[128,8]{0,1:T(8,128)}, u32[]{:S(2)}) copy-start(s32[128,8]{0,1:T(8,128)} %param.19) | copy-start | bytes 12292
  3.0 34.1 %copy-start.1 = (bf16[4,16,3072]{2,1,0:T(8,128)(2,1)S(1)}, bf16[4,16,3072]{2,1,0:T(8,128)(2,1)}, u32[]{:S(2)}) copy-start(bf16[4,16,3072]{2,1,0:T(8,128)(2,1)} %param.13) | copy-start | bytes 1179652
  3.7 78.1 %collective-permute-start.3 = (f32[64,4,128]{2,0,1:T(8,128)}, f32[64,4,128]{2,0,1:T(8,128)}, u32[]{:S(2)}, u32[]{:S(2)}) collective-permute-start(f32[64,4,128]{2,0,1:T(8,128)} %fusion.54), channel_id=1, source_target_pairs={{0,1},{1,0},{2,3},{3,2},{4,5},{5,4},{6,7},{7,6},{8,9},{9,8},{10,11... | collective-permute-start | bytes 393224 | tf_op jit(solution)/shard_map/ppermute | solution.py:18
  10.2 68.9 %collective-permute-start = (bf16[64,1,6,128]{3,0,2,1:T(8,128)(2,1)}, bf16[64,1,6,128]{3,0,2,1:T(8,128)(2,1)}, u32[]{:S(2)}, u32[]{:S(2)}) collective-permute-start(bf16[64,1,6,128]{3,0,2,1:T(8,128)(2,1)} %get-tuple-element.17), channel_id=1, source_target_pairs={{4,0},{8,4},{12,8},{16,12},{20,16},{24,20},{28,24},{32,28},{36,32}... | collective-permute-start | bytes 294920 | tf_op jit(solution)/shard_map/ppermute | solution.py:29
  13.1 78.6 %collective-permute-start.1 = (bf16[64,1,6,128]{3,0,2,1:T(8,128)(2,1)}, bf16[64,1,6,128]{3,0,2,1:T(8,128)(2,1)}, u32[]{:S(2)}, u32[]{:S(2)}) collective-permute-start(bf16[64,1,6,128]{3,0,2,1:T(8,128)(2,1)} %get-tuple-element.16), channel_id=1, source_target_pairs={{0,4},{4,8},{8,12},{12,16},{16,20},{20,24},{24,28},{28,32},{32,36}... | collective-permute-start | bytes 294920 | tf_op jit(solution)/shard_map/ppermute | solution.py:26
  18.0 0.9 copy-start.2
  19.6 72.0 %collective-permute-start.2 = (bf16[6,128,128]{2,1,0:T(8,128)(2,1)}, bf16[6,128,128]{2,1,0:T(8,128)(2,1)}, u32[]{:S(2)}, u32[]{:S(2)}) collective-permute-start(bf16[6,128,128]{2,1,0:T(8,128)(2,1)} %slice.135), channel_id=1, source_target_pairs={{0,4},{4,8},{8,12},{12,16},{16,20},{20,24},{24,28},{28,32},{32,36}... | collective-permute-start | bytes 589832 | tf_op jit(solution)/shard_map/ppermute | solution.py:14
  22.3 30.2 %all-to-all-start.1 = ((bf16[128,1,8]{2,1,0:T(2,128)(2,1)}), bf16[128,1,8]{2,1,0:T(2,128)(2,1)S(1)}, u32[]{:S(2)}, u32[]{:S(2)}) async-start(bf16[128,1,8]{2,1,0:T(2,128)(2,1)} %copy.130), calls=%async_computation.1 | async-start | bytes 131072 | tf_op jit(solution)/shard_map/all_to_all | solution.py:73
  35.6 7.5 %copy-start.15 = (s32[1024]{0:T(1024)}, s32[1024]{0:T(1024)S(1)}, u32[]{:S(2)}) copy-start(s32[1024]{0:T(1024)S(1)} %fusion.58) | copy-start | bytes 12292
  36.4 3.5 %copy-start.16 = (s32[1024]{0:T(1024)}, s32[1024]{0:T(1024)S(1)}, u32[]{:S(2)}) copy-start(s32[1024]{0:T(1024)S(1)} %fusion.57) | copy-start | bytes 12292
  50.4 24.3 %copy-start.3 = (bf16[24,128,128]{2,1,0:T(8,128)(2,1)S(1)}, bf16[24,128,128]{2,1,0:T(8,128)(2,1)}, u32[]{:S(2)}) copy-start(bf16[24,128,128]{2,1,0:T(8,128)(2,1)} %copy-done.2) | copy-start | bytes 2359300
  52.5 31.8 %all-to-all-start = ((bf16[128,2,512]{2,1,0:T(2,128)(2,1)}), bf16[128,2,512]{2,1,0:T(2,128)(2,1)}, u32[]{:S(2)}, u32[]{:S(2)}) async-start(bf16[128,2,512]{2,1,0:T(2,128)(2,1)} %reshape.304), calls=%async_computation | async-start | bytes 524288 | tf_op jit(solution)/shard_map/all_to_all | solution.py:107
  66.1 11.6 %collective-permute-start.5 = (bf16[128,8]{0,1:T(8,128)(2,1)}, bf16[128,8]{0,1:T(8,128)(2,1)}, u32[]{:S(2)}, u32[]{:S(2)}) collective-permute-start(bf16[128,8]{0,1:T(8,128)(2,1)} %bitcast.27), channel_id=1, source_target_pairs={{0,2},{1,3},{2,0},{3,1},{4,6},{5,7},{6,4},{7,5},{8,10},{9,11},{10,... | collective-permute-start | bytes 6152 | tf_op jit(solution)/shard_map/ppermute | solution.py:18
  74.6 2.5 copy-start.13
  81.8 9.9 %slice-start = ((f32[64,4,6,128]{3,0,2,1:T(8,128)}), f32[64,4,5,128]{3,0,2,1:T(8,128)S(1)}, s32[]{:S(2)}) async-start(f32[64,4,6,128]{3,0,2,1:T(8,128)} %copy-done.6), calls=%async_computation.3 | async-start | bytes 1310720 | tf_op jit(solution)/shard_map/slice | solution.py:96
  86.5 30.3 %collective-permute-start.4 = (bf16[64,128,16]{0,2,1:T(8,128)(2,1)}, bf16[64,128,16]{0,2,1:T(8,128)(2,1)}, u32[]{:S(2)}, u32[]{:S(2)}) collective-permute-start(bf16[64,128,16]{0,2,1:T(8,128)(2,1)} %bitcast.110), channel_id=1, source_target_pairs={{0,2},{1,3},{2,0},{3,1},{4,6},{5,7},{6,4},{7,5},{8,10},{9,11},{10,... | collective-permute-start | bytes 786440 | tf_op jit(solution)/shard_map/ppermute | solution.py:18
  158.0 1.9 copy-start.12
  158.0 1.9 copy-start.18
  158.0 2.1 copy-start.11
  158.0 2.1 copy-start.17
  160.2 27.8 %copy-start.5 = (f32[4,16,3072]{2,1,0:T(8,128)S(1)}, f32[4,16,3072]{2,1,0:T(8,128)}, u32[]{:S(2)}) copy-start(f32[4,16,3072]{2,1,0:T(8,128)} %get-tuple-element.9) | copy-start | bytes 2359300
  163.4 31.2 %all-to-all-start.2 = ((bf16[128,2,512]{2,1,0:T(2,128)(2,1)}), bf16[128,2,512]{2,1,0:T(2,128)(2,1)}, u32[]{:S(2)}, u32[]{:S(2)}) async-start(bf16[128,2,512]{2,1,0:T(2,128)(2,1)} %reshape.306), calls=%async_computation.2 | async-start | bytes 524288 | tf_op jit(solution)/shard_map/all_to_all | solution.py:107
  177.2 13.6 %collective-permute-start.6 = (bf16[64,1,6,128]{3,0,1,2:T(8,128)(2,1)}, bf16[64,1,6,128]{3,0,1,2:T(8,128)(2,1)S(1)}, u32[]{:S(2)}, u32[]{:S(2)}) collective-permute-start(bf16[64,1,6,128]{3,0,1,2:T(8,128)(2,1)} %get-tuple-element.13), channel_id=1, source_target_pairs={{4,0},{8,4},{12,8},{16,12},{20,16},{24,20},{28,24},{32,28},{36,32}... | collective-permute-start | bytes 294920 | tf_op jit(solution)/shard_map/ppermute | solution.py:29
  180.4 11.9 %collective-permute-start.8 = (f32[64,4,128]{2,0,1:T(8,128)S(1)}, f32[64,4,128]{2,0,1:T(8,128)S(1)}, u32[]{:S(2)}, u32[]{:S(2)}) collective-permute-start(f32[64,4,128]{2,0,1:T(8,128)S(1)} %fusion.53), channel_id=1, source_target_pairs={{0,1},{1,0},{2,3},{3,2},{4,5},{5,4},{6,7},{7,6},{8,9},{9,8},{10,11... | collective-permute-start | bytes 393224 | tf_op jit(solution)/shard_map/ppermute | solution.py:18
  182.4 19.2 %collective-permute-start.7 = (bf16[64,1,6,128]{3,0,1,2:T(8,128)(2,1)}, bf16[64,1,6,128]{3,0,1,2:T(8,128)(2,1)}, u32[]{:S(2)}, u32[]{:S(2)}) collective-permute-start(bf16[64,1,6,128]{3,0,1,2:T(8,128)(2,1)} %get-tuple-element.12), channel_id=1, source_target_pairs={{0,4},{4,8},{8,12},{12,16},{16,20},{20,24},{24,28},{28,32},{32,36}... | collective-permute-start | bytes 294920 | tf_op jit(solution)/shard_map/ppermute | solution.py:26
  188.8 1.1 copy-start.7
  188.8 2.1 copy-start.4
  196.7 31.3 %collective-permute-start.9 = (bf16[64,128,16]{0,2,1:T(8,128)(2,1)}, bf16[64,128,16]{0,2,1:T(8,128)(2,1)}, u32[]{:S(2)}, u32[]{:S(2)}) collective-permute-start(bf16[64,128,16]{0,2,1:T(8,128)(2,1)} %bitcast.112), channel_id=1, source_target_pairs={{0,2},{1,3},{2,0},{3,1},{4,6},{5,7},{6,4},{7,5},{8,10},{9,11},{10,... | collective-permute-start | bytes 786440 | tf_op jit(solution)/shard_map/ppermute | solution.py:18
  203.8 33.6 %copy-start.14 = (f32[1024]{0:T(1024)S(1)}, f32[1024]{0:T(1024)}, u32[]{:S(2)}) copy-start(f32[1024]{0:T(1024)} %reshape.217) | copy-start | bytes 12292
  246.9 1.9 copy-start.8
  246.9 1.9 copy-start.19
where the time goes:
time: 252 us; the launch traced here: 251 us
  starting transfers between devices  82.9 us (33%)
  local copies, waits for them, and re-layouts  55.3 us (22%)
  other arithmetic  52.2 us (21%)
  waiting for transfers between devices  43.1 us (17%)
  matrix products  16 us (6%)
    ppermute x5, waiting for transfers between devices, partner_2(): lax.ppermute(value, axis, [(i, i ^ 1 << bit) for i in range(lax.axis_size...  43.1 us
    all_to_all x2, starting transfers between devices, apply_hop(): lax.all_to_all(paired, 'tile', split_axis=1, concat_axis=1, tiled=True)  26.7 us
    ppermute x5, starting transfers between devices, partner_2(): lax.ppermute(value, axis, [(i, i ^ 1 << bit) for i in range(lax.axis_size...  25.6 us
    scatter-add x2, other arithmetic, apply_hop(): accumulated = accumulated.at[:, send_rows].add(returned_terms)  16.9 us
    scatter-add x2, other arithmetic, apply_hop(): accumulated = accumulated.at[:, recv_sites].add(arrived_terms)  16.6 us
    all_to_all x1, starting transfers between devices, shards(): lax.all_to_all(weight_table, 'tile', split_axis=0, concat_axis=0, tiled=T...  13.1 us
    ppermute x2, starting transfers between devices, with_halo(): lax.ppermute(lax.slice_in_dim(block, block.shape[dim] - width, None, axis...  10.4 us
    unnamed x56, local copies, waits for them, and re-layouts  10.2 us
  transfers between devices with their start and end apart: 13, of which 2 were waited for; matrix products, arithmetic and copies ran while one was open for 20% of the time, Pallas kernels for 0%

commit v1 on v0

--- a/solution.py
+++ b/solution.py
@@ -2,6 +2,7 @@
 import jax.numpy as jnp
 from jax import lax
 from jax.sharding import PartitionSpec as P
+from jax.lax import all_to_all, axis_size
 
 TILE = 128
 TR = 4
@@ -104,7 +105,16 @@
             field_rows, tile_count, slot_count
         )
         paired = jnp.concatenate([outgoing, own_ends], axis=2)
-        paired_spread = lax.all_to_all(paired, "tile", split_axis=1, concat_axis=1, tiled=True)
+        order_corner_in = lambda state: jnp.concatenate(
+            all_to_all(
+                jnp.stack(jnp.split(state, axis_size("tile"), axis=1), axis=0),
+                axis_name="tile",
+                split_axis=0,
+                concat_axis=0,
+            ),
+            axis=1,
+        )
+        paired_spread = order_corner_in(paired)
         landed = partner_2(paired_spread, "layer", 1)
         arrived_terms = (
             landed[:, :, :slot_count].reshape(field_rows, -1).astype(jnp.float32)

time: 252 us -> 259 us (1.028)
  local copies, waits for them, and re-layouts: 55.3 us -> 58.9 us
  waiting for transfers between devices: 43.1 us -> 40.2 us
    ppermute x5, waiting for transfers between devices: 43.1 us -> 40.2 us  [partner_2(): lax.ppermute(value, axis, [(i, i ^ 1 << bit) for i in range(lax.axis_size...]
    reshape x0 -> x2, local copies, waits for them, and re-layouts: none -> 2.73 us  [apply_hop(): jnp.concatenate(all_to_all(jnp.stack(jnp.split(state, axis_size('tile'),...]
    unnamed x56 -> x62, local copies, waits for them, and re-layouts: 10.2 us -> 10.9 us
  transfers between devices with their start and end apart: 13 -> 13, of which waited for: 2 -> 2; matrix products, arithmetic and copies ran while one was open for 20% -> 21% of each run, Pallas kernels for 0% -> 0%
where the time goes in v1:
time: 259 us; the launch traced here: 256 us
  starting transfers between devices  83.1 us (32%)
  local copies, waits for them, and re-layouts  58.9 us (23%)
  other arithmetic  54.7 us (21%)
  waiting for transfers between devices  40.2 us (16%)
  matrix products  16.7 us (6%)
    ppermute x5, waiting for transfers between devices, partner_2(): lax.ppermute(value, axis, [(i, i ^ 1 << bit) for i in range(lax.axis_size...  40.2 us
    all_to_all x2, starting transfers between devices, apply_hop(): all_to_all(jnp.stack(jnp.split(state, axis_size('tile'), axis=1), axis=0)...  26.8 us
    ppermute x5, starting transfers between devices, partner_2(): lax.ppermute(value, axis, [(i, i ^ 1 << bit) for i in range(lax.axis_size...  25.7 us
    scatter-add x2, other arithmetic, apply_hop(): accumulated = accumulated.at[:, send_rows].add(returned_terms)  16.9 us
    scatter-add x2, other arithmetic, apply_hop(): accumulated = accumulated.at[:, recv_sites].add(arrived_terms)  16.5 us
    all_to_all x1, starting transfers between devices, shards(): lax.all_to_all(weight_table, 'tile', split_axis=0, concat_axis=0, tiled=T...  13.1 us
    unnamed x62, local copies, waits for them, and re-layouts  10.9 us
    ppermute x2, starting transfers between devices, with_halo(): lax.ppermute(lax.slice_in_dim(block, block.shape[dim] - width, None, axis...  10.4 us
  transfers between devices with their start and end apart: 13, of which 2 were waited for; matrix products, arithmetic and copies ran while one was open for 21% of the time, Pallas kernels for 0%

profile of v1, /device:TPU:7, one launch (start us, length us, event | category | flops | bytes accessed | tf_op | source)
XLA Modules:
  0.0 255.7 jit_solution(4230194438224088174)
XLA Ops:
  0.7 1.6 reshape.209
  3.7 5.8 %collective-permute-start.3 = (f32[64,4,128]{2,0,1:T(8,128)}, f32[64,4,128]{2,0,1:T(8,128)}, u32[]{:S(2)}, u32[]{:S(2)}) collective-permute-start(f32[64,4,128]{2,0,1:T(8,128)} %fusion.54), channel_id=1, source_target_pairs={{0,1},{1,0},{2,3},{3,2},{4,5},{5,4},{6,7},{7,6},{8,9},{9,8},{10,11... | collective-permute-start | bytes 393224 | tf_op jit(solution)/shard_map/ppermute | solution.py:19
  10.2 2.9 %collective-permute-start = (bf16[64,1,6,128]{3,0,2,1:T(8,128)(2,1)}, bf16[64,1,6,128]{3,0,2,1:T(8,128)(2,1)}, u32[]{:S(2)}, u32[]{:S(2)}) collective-permute-start(bf16[64,1,6,128]{3,0,2,1:T(8,128)(2,1)} %get-tuple-element.17), channel_id=1, source_target_pairs={{4,0},{8,4},{12,8},{16,12},{20,16},{24,20},{28,24},{32,28},{36,32}... | collective-permute-start | bytes 294920 | tf_op jit(solution)/shard_map/ppermute | solution.py:30
  13.1 4.8 %collective-permute-start.1 = (bf16[64,1,6,128]{3,0,2,1:T(8,128)(2,1)}, bf16[64,1,6,128]{3,0,2,1:T(8,128)(2,1)}, u32[]{:S(2)}, u32[]{:S(2)}) collective-permute-start(bf16[64,1,6,128]{3,0,2,1:T(8,128)(2,1)} %get-tuple-element.16), channel_id=1, source_target_pairs={{0,4},{4,8},{8,12},{12,16},{16,20},{20,24},{24,28},{28,32},{32,36}... | collective-permute-start | bytes 294920 | tf_op jit(solution)/shard_map/ppermute | solution.py:27
  19.6 1.9 collective-permute-start.2
  22.3 13.1 %all-to-all-start.1 = ((bf16[128,1,8]{2,1,0:T(2,128)(2,1)}), bf16[128,1,8]{2,1,0:T(2,128)(2,1)S(1)}, u32[]{:S(2)}, u32[]{:S(2)}) async-start(bf16[128,1,8]{2,1,0:T(2,128)(2,1)} %copy.130), calls=%async_computation.1 | async-start | bytes 131072 | tf_op jit(solution)/shard_map/all_to_all | solution.py:74
  38.4 3.2 %gather_fusion.1 = bf16[1024,64]{1,0:T(8,128)(2,1)S(1)} fusion(bf16[64,3072]{0,1:T(8,128)(2,1)S(1)} %copy.124, s32[1024]{0:T(1024)S(1)} %get-tuple-element.23), kind=kCustom, calls=%fused_computation.1.clone | custom fusion | bytes 266240 | tf_op jit(solution)/shard_map/jit(_take)/gather | solution.py:104
  41.7 4.3 %gather_fusion = bf16[1024,64]{1,0:T(8,128)(2,1)} fusion(bf16[64,3072]{0,1:T(8,128)(2,1)S(1)} %copy.124, s32[1024]{0:T(1024)S(1)} %get-tuple-element.22), kind=kCustom, calls=%fused_computation.clone | custom fusion | bytes 266240 | tf_op jit(solution)/shard_map/jit(_take)/gather | solution.py:101
  49.9 1.5 fusion.326
  52.8 2.1 reshape.320
  55.0 12.9 %all-to-all-start = ((bf16[128,2,512]{2,1,0:T(2,128)(2,1)}), bf16[128,2,512]{2,1,0:T(2,128)(2,1)}, u32[]{:S(2)}, u32[]{:S(2)}) async-start(bf16[128,2,512]{2,1,0:T(2,128)(2,1)} %reshape.320), calls=%async_computation | async-start | bytes 524288 | tf_op jit(solution)/shard_map/all_to_all | solution.py:109
  68.5 7.9 %collective-permute-start.5 = (bf16[128,8]{0,1:T(8,128)(2,1)}, bf16[128,8]{0,1:T(8,128)(2,1)}, u32[]{:S(2)}, u32[]{:S(2)}) collective-permute-start(bf16[128,8]{0,1:T(8,128)(2,1)} %bitcast.157), channel_id=1, source_target_pairs={{0,2},{1,3},{2,0},{3,1},{4,6},{5,7},{6,4},{7,5},{8,10},{9,11},{10,... | collective-permute-start | bytes 6152 | tf_op jit(solution)/shard_map/ppermute | solution.py:19
  81.5 2.7 %convolution_add_fusion.3 = f32[4,6,64,128]{3,2,1,0:T(8,128)} fusion(f32[4,6,64,128]{3,2,1,0:T(8,128)} %fusion.326, bf16[4,6,128,128]{3,2,1,0:T(8,128)(2,1)S(1)} %bitcast.657, bf16[64,1,6,128]{3,0,2,1:T(8,128)(2,1)} %collective-permute-done, bf16[64,4,6,128]{3,0,2,1:T(8,128)(2,1)S(1)} %copy.110), kind=kOutput, calls=%fused_computation.528 | convolution fusion | flops 51511296 | bytes 2850816 | tf_op jit(solution)/shard_map/rkij,nrkj->nrki/dot_general | solution.py:36
  85.8 1.5 fusion.42
  87.3 1.3 reshape.321
  89.5 5.2 %collective-permute-start.4 = (bf16[64,128,16]{0,2,1:T(8,128)(2,1)}, bf16[64,128,16]{0,2,1:T(8,128)(2,1)}, u32[]{:S(2)}, u32[]{:S(2)}) collective-permute-start(bf16[64,128,16]{0,2,1:T(8,128)(2,1)} %bitcast_bitcast_fusion.1), channel_id=1, source_target_pairs={{0,2},{1,3},{2,0},{3,1},{4,6},{5,7},{6,4},{7,5},{8,10},{9,11},{10,... | collective-permute-start | bytes 786440 | tf_op jit(solution)/shard_map/ppermute | solution.py:19
  94.7 2.9 %fusion.5 = f32[64,4,6,128]{3,0,2,1:T(8,128)} fusion(f32[4,6,64,128]{3,2,1,0:T(8,128)} %fusion.42, f32[4,6,64,128]{3,2,1,0:T(8,128)} %convolution_add_fusion.3, f32[64,4,5,128]{3,0,2,1:T(8,128)S(1)} %slice-done, f32[64,4,1,128]{3,0,2,1:T(8,128)} %select_bitcast_fusion.5, bf16[64,4,6,128]{3,0,2,1:T(8,128)(2,1)S(1)} %copy.110, ...), kind=kOutput, calls=%fused_computation.527 | convolution fusion | flops 53673984 | bytes 4423680 | tf_op jit(solution)/shard_map/rkji,nrkj->nrki/dot_general | solution.py:40
  97.6 1.6 copy.166
  99.2 20.5 %collective-permute-done.4 = bf16[64,128,16]{0,2,1:T(8,128)(2,1)} collective-permute-done((bf16[64,128,16]{0,2,1:T(8,128)(2,1)}, bf16[64,128,16]{0,2,1:T(8,128)(2,1)}, u32[]{:S(2)}, u32[]{:S(2)}) %collective-permute-start.4) | collective-permute-done | bytes 262176 | tf_op jit(solution)/shard_map/ppermute | solution.py:19
  119.7 7.1 %scatter_custom_fusion = f32[64,3072]{0,1:T(8,128)S(1)} fusion(f32[64,3072]{0,1:T(8,128)S(1)} %bitcast.650, s32[1024]{0:T(1024)} %bitcast.666, bf16[64,128,16]{0,2,1:T(8,128)(2,1)} %collective-permute-done.4, f32[1024]{0:T(1024)S(1)} %mul.125), kind=kCustom, calls=%fused_computation.816 | custom fusion | flops 196608 | bytes 1052672 | tf_op jit(solution)/shard_map/scatter-add | solution.py:123
  126.8 7.5 %scatter_custom_fusion.1 = f32[64,3072]{0,1:T(8,128)S(1)} fusion(f32[64,3072]{0,1:T(8,128)S(1)} %scatter_custom_fusion, s32[1024]{0:T(1024)} %bitcast.668, bf16[64,128,16]{0,2,1:T(8,128)(2,1)} %collective-permute-done.4, f32[1024]{0:T(1024)} %reshape.233), kind=kCustom, calls=%fused_computation.813 | custom fusion | flops 196608 | bytes 1052672 | tf_op jit(solution)/shard_map/scatter-add | solution.py:128
  134.3 1.3 copy.133
  135.6 2.6 %pad_maximum_fusion.1 = (f32[4,16,3072]{2,1,0:T(8,128)}, f32[4,16,3072]{2,1,0:T(8,128)}) fusion(f32[2,16,3072]{2,1,0:T(8,128)} %get-tuple-element.15, f32[2,16,3072]{2,1,0:T(8,128)} %get-tuple-element.14, f32[3072]{0:T(1024)S(1)} %copy-done.15, f32[4,16,3072]{2,1,0:T(8,128)} %bitcast.661, f32[4]{0:T(128)} %constant.42.clone), kind=kLoop, calls=%fused_computation.530 | loop fusion | flops 786432 | bytes 3158032 | tf_op jit(solution)/shard_map/jit(_roll_static)/concatenate | solution.py:133
  138.3 2.8 %copy.149 = f32[64,3072]{0,1:T(8,128)} copy(f32[64,3072]{1,0:T(8,128)} %bitcast.659) | data formatting | bytes 1572864 | tf_op jit(solution)/shard_map/jit(_roll_static)/concatenate | solution.py:133
  141.0 2.8 %add_convert_fusion = bf16[64,3072]{0,1:T(8,128)(2,1)} fusion(f32[64,3072]{0,1:T(8,128)} %copy.149, f32[64,3072]{0,1:T(8,128)S(1)} %scatter_custom_fusion.1, f32[3072]{0:T(1024)S(1)} %copy-done.15, f32[64]{0:T(128)} %mul.136), kind=kLoop, calls=%fused_computation.516 | loop fusion | flops 786432 | bytes 1978624 | tf_op jit(solution)/shard_map/convert_element_type | solution.py:134
  143.8 5.7 %gather_fusion.2 = bf16[1024,64]{1,0:T(8,128)(2,1)} fusion(bf16[64,3072]{0,1:T(8,128)(2,1)} %add_convert_fusion, s32[1024]{0:T(1024)} %copy-done.18), kind=kCustom, calls=%fused_computation.2.clone | custom fusion | bytes 266240 | tf_op jit(solution)/shard_map/jit(_take)/gather | solution.py:101
  149.5 5.6 %gather_fusion.3 = bf16[1024,64]{1,0:T(8,128)(2,1)} fusion(bf16[64,3072]{0,1:T(8,128)(2,1)} %add_convert_fusion, s32[1024]{0:T(1024)} %copy-done.17), kind=kCustom, calls=%fused_computation.3.clone | custom fusion | bytes 266240 | tf_op jit(solution)/shard_map/jit(_take)/gather | solution.py:104
  155.1 2.5 concatenate.53
  157.6 1.3 copy.135
  159.0 2.0 fusion.14
  161.7 1.2 convolution_bitcast_fusion.1
  166.0 2.1 reshape.322
  168.1 14.0 %all-to-all-start.2 = ((bf16[128,2,512]{2,1,0:T(2,128)(2,1)}), bf16[128,2,512]{2,1,0:T(2,128)(2,1)}, u32[]{:S(2)}, u32[]{:S(2)}) async-start(bf16[128,2,512]{2,1,0:T(2,128)(2,1)} %reshape.322), calls=%async_computation.2 | async-start | bytes 524288 | tf_op jit(solution)/shard_map/all_to_all | solution.py:109
  182.1 2.3 collective-permute-start.6
  185.3 1.9 collective-permute-start.8
  187.2 5.6 %collective-permute-start.7 = (bf16[64,1,6,128]{3,0,1,2:T(8,128)(2,1)}, bf16[64,1,6,128]{3,0,1,2:T(8,128)(2,1)}, u32[]{:S(2)}, u32[]{:S(2)}) collective-permute-start(bf16[64,1,6,128]{3,0,1,2:T(8,128)(2,1)} %get-tuple-element.12), channel_id=1, source_target_pairs={{0,4},{4,8},{8,12},{12,16},{16,20},{20,24},{24,28},{28,32},{32,36}... | collective-permute-start | bytes 294920 | tf_op jit(solution)/shard_map/ppermute | solution.py:27
  194.8 1.5 convolution_add_fusion.1
  197.0 1.5 fusion.15
  198.5 2.2 reshape.323
  200.7 1.9 bitcast_bitcast_fusion
  202.6 4.9 %collective-permute-start.9 = (bf16[64,128,16]{0,2,1:T(8,128)(2,1)}, bf16[64,128,16]{0,2,1:T(8,128)(2,1)}, u32[]{:S(2)}, u32[]{:S(2)}) collective-permute-start(bf16[64,128,16]{0,2,1:T(8,128)(2,1)} %bitcast_bitcast_fusion), channel_id=1, source_target_pairs={{0,2},{1,3},{2,0},{3,1},{4,6},{5,7},{6,4},{7,5},{8,10},{9,11},{10,... | collective-permute-start | bytes 786440 | tf_op jit(solution)/shard_map/ppermute | solution.py:19
  207.5 2.9 %fusion.2 = f32[64,4,6,128]{3,0,1,2:T(8,128)} fusion(f32[4,6,64,128]{3,2,0,1:T(8,128)} %fusion.15, f32[4,6,64,128]{3,2,0,1:T(8,128)} %convolution_add_fusion.1, f32[64,4,5,128]{3,0,1,2:T(8,128)S(1)} %slice-done.1, f32[64,4,1,128]{3,0,1,2:T(8,128)S(1)} %copy-done.14, bf16[64,4,6,128]{3,0,1,2:T(8,128)(2,1)S(1)} %fusion.14, ...), kind=kOutput, calls=%fused_computation.522 | convolution fusion | flops 52494336 | bytes 4423680 | tf_op jit(solution)/shard_map/rkji,nrkj->nrki/dot_general | solution.py:40
  210.4 2.8 %copy.169 = f32[64,4,6,128]{0,3,2,1:T(8,128)} copy(f32[64,4,6,128]{3,0,1,2:T(8,128)} %fusion.2) | data formatting | bytes 1572864 | tf_op jit(solution)/shard_map/reshape | solution.py:99
  213.2 19.7 %collective-permute-done.9 = bf16[64,128,16]{0,2,1:T(8,128)(2,1)} collective-permute-done((bf16[64,128,16]{0,2,1:T(8,128)(2,1)}, bf16[64,128,16]{0,2,1:T(8,128)(2,1)}, u32[]{:S(2)}, u32[]{:S(2)}) %collective-permute-start.9) | collective-permute-done | bytes 262176 | tf_op jit(solution)/shard_map/ppermute | solution.py:19
  232.9 9.4 %scatter_custom_fusion.2 = f32[64,3072]{0,1:T(8,128)} fusion(f32[64,3072]{0,1:T(8,128)} %bitcast.660, s32[1024]{0:T(1024)} %bitcast.667, bf16[64,128,16]{0,2,1:T(8,128)(2,1)} %collective-permute-done.9, f32[1024]{0:T(1024)S(1)} %mul.125), kind=kCustom, calls=%fused_computation.810 | custom fusion | flops 196608 | bytes 1052672 | tf_op jit(solution)/shard_map/scatter-add | solution.py:123
  242.3 9.4 %scatter_custom_fusion.3 = f32[64,3072]{0,1:T(8,128)} fusion(f32[64,3072]{0,1:T(8,128)} %scatter_custom_fusion.2, s32[1024]{0:T(1024)} %bitcast.669, bf16[64,128,16]{0,2,1:T(8,128)(2,1)} %collective-permute-done.9, f32[1024]{0:T(1024)S(1)} %copy-done.16), kind=kCustom, calls=%fused_computation.807 | custom fusion | flops 196608 | bytes 1052672 | tf_op jit(solution)/shard_map/scatter-add | solution.py:128
  251.8 1.9 copy.151
  253.7 1.2 multiply_reduce_fusion.2
  (380 shorter events, 28.4 us)
Async XLA Ops:
  0.6 49.3 %copy-start = (bf16[24,128,128]{2,1,0:T(8,128)(2,1)S(1)}, bf16[24,128,128]{2,1,0:T(8,128)(2,1)}, u32[]{:S(2)}) copy-start(bf16[24,128,128]{2,1,0:T(8,128)(2,1)} %param.14) | copy-start | bytes 2359300
  0.6 1.8 copy-start.27
  0.7 1.8 copy-start.8
  2.6 15.3 %copy-start.9 = (bf16[24,128,128]{2,1,0:T(8,128)(2,1)S(1)}, bf16[24,128,128]{2,1,0:T(8,128)(2,1)}, u32[]{:S(2)}) copy-start(bf16[24,128,128]{2,1,0:T(8,128)(2,1)} %param.15) | copy-start | bytes 2359300
  3.0 14.9 %copy-start.6 = (f32[64,4,6,128]{3,0,2,1:T(8,128)}, f32[64,4,6,128]{3,0,2,1:T(8,128)S(1)}, u32[]{:S(2)}) copy-start(f32[64,4,6,128]{3,0,2,1:T(8,128)S(1)} %convolution_bitcast_fusion) | copy-start | bytes 2359300
  3.0 18.6 %copy-start.25 = (bf16[128,8]{0,1:T(8,128)(2,1)S(1)}, bf16[128,8]{0,1:T(8,128)(2,1)}, u32[]{:S(2)}) copy-start(bf16[128,8]{0,1:T(8,128)(2,1)} %param.21) | copy-start | bytes 6148
  3.0 18.6 %copy-start.26 = (s32[128]{0:T(128)S(1)}, s32[128]{0:T(128)}, u32[]{:S(2)}) copy-start(s32[128]{0:T(128)} %param.22) | copy-start | bytes 1540
  3.0 32.4 %copy-start.23 = (s32[128,8]{0,1:T(8,128)S(1)}, s32[128,8]{0,1:T(8,128)}, u32[]{:S(2)}) copy-start(s32[128,8]{0,1:T(8,128)} %param.19) | copy-start | bytes 12292
  3.0 32.6 %copy-start.24 = (s32[128,8]{0,1:T(8,128)S(1)}, s32[128,8]{0,1:T(8,128)}, u32[]{:S(2)}) copy-start(s32[128,8]{0,1:T(8,128)} %param.20) | copy-start | bytes 12292
  3.0 34.1 %copy-start.1 = (bf16[4,16,3072]{2,1,0:T(8,128)(2,1)S(1)}, bf16[4,16,3072]{2,1,0:T(8,128)(2,1)}, u32[]{:S(2)}) copy-start(bf16[4,16,3072]{2,1,0:T(8,128)(2,1)} %param.13) | copy-start | bytes 1179652
  3.7 80.5 %collective-permute-start.3 = (f32[64,4,128]{2,0,1:T(8,128)}, f32[64,4,128]{2,0,1:T(8,128)}, u32[]{:S(2)}, u32[]{:S(2)}) collective-permute-start(f32[64,4,128]{2,0,1:T(8,128)} %fusion.54), channel_id=1, source_target_pairs={{0,1},{1,0},{2,3},{3,2},{4,5},{5,4},{6,7},{7,6},{8,9},{9,8},{10,11... | collective-permute-start | bytes 393224 | tf_op jit(solution)/shard_map/ppermute | solution.py:19
  10.2 71.3 %collective-permute-start = (bf16[64,1,6,128]{3,0,2,1:T(8,128)(2,1)}, bf16[64,1,6,128]{3,0,2,1:T(8,128)(2,1)}, u32[]{:S(2)}, u32[]{:S(2)}) collective-permute-start(bf16[64,1,6,128]{3,0,2,1:T(8,128)(2,1)} %get-tuple-element.17), channel_id=1, source_target_pairs={{4,0},{8,4},{12,8},{16,12},{20,16},{24,20},{28,24},{32,28},{36,32}... | collective-permute-start | bytes 294920 | tf_op jit(solution)/shard_map/ppermute | solution.py:30
  13.1 81.7 %collective-permute-start.1 = (bf16[64,1,6,128]{3,0,2,1:T(8,128)(2,1)}, bf16[64,1,6,128]{3,0,2,1:T(8,128)(2,1)}, u32[]{:S(2)}, u32[]{:S(2)}) collective-permute-start(bf16[64,1,6,128]{3,0,2,1:T(8,128)(2,1)} %get-tuple-element.16), channel_id=1, source_target_pairs={{0,4},{4,8},{8,12},{12,16},{16,20},{20,24},{24,28},{28,32},{32,36}... | collective-permute-start | bytes 294920 | tf_op jit(solution)/shard_map/ppermute | solution.py:27
  18.0 0.9 copy-start.2
  19.6 75.1 %collective-permute-start.2 = (bf16[6,128,128]{2,1,0:T(8,128)(2,1)}, bf16[6,128,128]{2,1,0:T(8,128)(2,1)}, u32[]{:S(2)}, u32[]{:S(2)}) collective-permute-start(bf16[6,128,128]{2,1,0:T(8,128)(2,1)} %slice.135), channel_id=1, source_target_pairs={{0,4},{4,8},{8,12},{12,16},{16,20},{20,24},{24,28},{28,32},{32,36}... | collective-permute-start | bytes 589832 | tf_op jit(solution)/shard_map/ppermute | solution.py:15
  22.3 32.6 %all-to-all-start.1 = ((bf16[128,1,8]{2,1,0:T(2,128)(2,1)}), bf16[128,1,8]{2,1,0:T(2,128)(2,1)S(1)}, u32[]{:S(2)}, u32[]{:S(2)}) async-start(bf16[128,1,8]{2,1,0:T(2,128)(2,1)} %copy.130), calls=%async_computation.1 | async-start | bytes 131072 | tf_op jit(solution)/shard_map/all_to_all | solution.py:74
  36.4 5.2 %copy-start.17 = (s32[1024]{0:T(1024)}, s32[1024]{0:T(1024)S(1)}, u32[]{:S(2)}) copy-start(s32[1024]{0:T(1024)S(1)} %get-tuple-element.23) | copy-start | bytes 12292
  36.4 5.2 %copy-start.18 = (s32[1024]{0:T(1024)}, s32[1024]{0:T(1024)S(1)}, u32[]{:S(2)}) copy-start(s32[1024]{0:T(1024)S(1)} %get-tuple-element.22) | copy-start | bytes 12292
  41.6 5.2 %copy-start.20 = (pred[1024]{0:T(1024)(128)(4,1)S(1)}, pred[1024]{0:T(1024)(128)(4,1)}, u32[]{:S(2)}) copy-start(pred[1024]{0:T(1024)(128)(4,1)} %compare_and_fusion.1) | copy-start | bytes 3076
  52.0 0.8 copy-start.12
  52.8 24.2 %copy-start.3 = (bf16[24,128,128]{2,1,0:T(8,128)(2,1)S(1)}, bf16[24,128,128]{2,1,0:T(8,128)(2,1)}, u32[]{:S(2)}) copy-start(bf16[24,128,128]{2,1,0:T(8,128)(2,1)} %copy-done.2) | copy-start | bytes 2359300
  55.0 32.4 %all-to-all-start = ((bf16[128,2,512]{2,1,0:T(2,128)(2,1)}), bf16[128,2,512]{2,1,0:T(2,128)(2,1)}, u32[]{:S(2)}, u32[]{:S(2)}) async-start(bf16[128,2,512]{2,1,0:T(2,128)(2,1)} %reshape.320), calls=%async_computation | async-start | bytes 524288 | tf_op jit(solution)/shard_map/all_to_all | solution.py:109
  68.5 11.6 %collective-permute-start.5 = (bf16[128,8]{0,1:T(8,128)(2,1)}, bf16[128,8]{0,1:T(8,128)(2,1)}, u32[]{:S(2)}, u32[]{:S(2)}) collective-permute-start(bf16[128,8]{0,1:T(8,128)(2,1)} %bitcast.157), channel_id=1, source_target_pairs={{0,2},{1,3},{2,0},{3,1},{4,6},{5,7},{6,4},{7,5},{8,10},{9,11},{10,... | collective-permute-start | bytes 6152 | tf_op jit(solution)/shard_map/ppermute | solution.py:19
  77.0 2.4 copy-start.15
  85.8 8.9 %slice-start = ((f32[64,4,6,128]{3,0,2,1:T(8,128)}), f32[64,4,5,128]{3,0,2,1:T(8,128)S(1)}, s32[]{:S(2)}) async-start(f32[64,4,6,128]{3,0,2,1:T(8,128)} %copy-done.6), calls=%async_computation.3 | async-start | bytes 1310720 | tf_op jit(solution)/shard_map/slice | solution.py:97
  89.5 30.2 %collective-permute-start.4 = (bf16[64,128,16]{0,2,1:T(8,128)(2,1)}, bf16[64,128,16]{0,2,1:T(8,128)(2,1)}, u32[]{:S(2)}, u32[]{:S(2)}) collective-permute-start(bf16[64,128,16]{0,2,1:T(8,128)(2,1)} %bitcast_bitcast_fusion.1), channel_id=1, source_target_pairs={{0,2},{1,3},{2,0},{3,1},{4,6},{5,7},{6,4},{7,5},{8,10},{9,11},{10,... | collective-permute-start | bytes 786440 | tf_op jit(solution)/shard_map/ppermute | solution.py:19
  160.9 1.9 copy-start.11
  160.9 1.9 copy-start.21
  160.9 2.1 copy-start.10
  161.0 2.1 copy-start.19
  165.2 27.7 %copy-start.5 = (f32[4,16,3072]{2,1,0:T(8,128)S(1)}, f32[4,16,3072]{2,1,0:T(8,128)}, u32[]{:S(2)}) copy-start(f32[4,16,3072]{2,1,0:T(8,128)} %get-tuple-element.9) | copy-start | bytes 2359300
  165.2 0.8 copy-start.13
  168.1 30.4 %all-to-all-start.2 = ((bf16[128,2,512]{2,1,0:T(2,128)(2,1)}), bf16[128,2,512]{2,1,0:T(2,128)(2,1)}, u32[]{:S(2)}, u32[]{:S(2)}) async-start(bf16[128,2,512]{2,1,0:T(2,128)(2,1)} %reshape.322), calls=%async_computation.2 | async-start | bytes 524288 | tf_op jit(solution)/shard_map/all_to_all | solution.py:109
  182.1 12.2 %collective-permute-start.6 = (bf16[64,1,6,128]{3,0,1,2:T(8,128)(2,1)}, bf16[64,1,6,128]{3,0,1,2:T(8,128)(2,1)S(1)}, u32[]{:S(2)}, u32[]{:S(2)}) collective-permute-start(bf16[64,1,6,128]{3,0,1,2:T(8,128)(2,1)} %get-tuple-element.13), channel_id=1, source_target_pairs={{4,0},{8,4},{12,8},{16,12},{20,16},{24,20},{28,24},{32,28},{36,32}... | collective-permute-start | bytes 294920 | tf_op jit(solution)/shard_map/ppermute | solution.py:30
  185.3 11.0 %collective-permute-start.8 = (f32[64,4,128]{2,0,1:T(8,128)S(1)}, f32[64,4,128]{2,0,1:T(8,128)S(1)}, u32[]{:S(2)}, u32[]{:S(2)}) collective-permute-start(f32[64,4,128]{2,0,1:T(8,128)S(1)} %fusion.53), channel_id=1, source_target_pairs={{0,1},{1,0},{2,3},{3,2},{4,5},{5,4},{6,7},{7,6},{8,9},{9,8},{10,11... | collective-permute-start | bytes 393224 | tf_op jit(solution)/shard_map/ppermute | solution.py:19
  187.2 20.3 %collective-permute-start.7 = (bf16[64,1,6,128]{3,0,1,2:T(8,128)(2,1)}, bf16[64,1,6,128]{3,0,1,2:T(8,128)(2,1)}, u32[]{:S(2)}, u32[]{:S(2)}) collective-permute-start(bf16[64,1,6,128]{3,0,1,2:T(8,128)(2,1)} %get-tuple-element.12), channel_id=1, source_target_pairs={{0,4},{4,8},{8,12},{12,16},{16,20},{20,24},{24,28},{28,32},{32,36}... | collective-permute-start | bytes 294920 | tf_op jit(solution)/shard_map/ppermute | solution.py:27
  193.6 1.1 copy-start.4
  198.5 9.0 %slice-start.1 = ((f32[64,4,6,128]{3,0,1,2:T(8,128)}), f32[64,4,5,128]{3,0,1,2:T(8,128)S(1)}, s32[]{:S(2)}) async-start(f32[64,4,6,128]{3,0,1,2:T(8,128)} %convolution_bitcast_fusion.1), calls=%async_computation.4 | async-start | bytes 1310720 | tf_op jit(solution)/shard_map/slice | solution.py:97
  198.5 9.0 %copy-start.14 = (f32[64,4,1,128]{3,0,1,2:T(8,128)S(1)}, f32[64,4,1,128]{3,0,1,2:T(8,128)}, u32[]{:S(2)}) copy-start(f32[64,4,1,128]{3,0,1,2:T(8,128)} %select_bitcast_fusion.4) | copy-start | bytes 393220
  202.6 30.3 %collective-permute-start.9 = (bf16[64,128,16]{0,2,1:T(8,128)(2,1)}, bf16[64,128,16]{0,2,1:T(8,128)(2,1)}, u32[]{:S(2)}, u32[]{:S(2)}) collective-permute-start(bf16[64,128,16]{0,2,1:T(8,128)(2,1)} %bitcast_bitcast_fusion), channel_id=1, source_target_pairs={{0,2},{1,3},{2,0},{3,1},{4,6},{5,7},{6,4},{7,5},{8,10},{9,11},{10,... | collective-permute-start | bytes 786440 | tf_op jit(solution)/shard_map/ppermute | solution.py:19
  210.4 31.9 %copy-start.16 = (f32[1024]{0:T(1024)S(1)}, f32[1024]{0:T(1024)}, u32[]{:S(2)}) copy-start(f32[1024]{0:T(1024)} %reshape.233) | copy-start | bytes 12292
  251.8 1.9 copy-start.7
  251.8 1.9 copy-start.22
